TPU v7x, 512 devices: a whole 4x8x8 slice. The times are simulated.
512 devices in a mesh: row: 32 (over y, x), head: 16 (over z, core).
Axes of the slice: x: 4, y: 8, z: 8, core: 2. Of those that a mesh axis runs over, the one named last changes fastest.
Arguments:
- patches: bfloat16 [196608, 768], P(('row', 'head')), may hold values from -6 to 6
- w_patch: bfloat16 [768, 1024], replicated, may hold values from -0.21875 to 0.21875
- patch_bias: float32 [1024], replicated, may hold values from -4 to 4
- w_kv: bfloat16 [1024, 2048], P(None, 'head'), may hold values from -0.1875 to 0.1875
- queries: bfloat16 [2048, 1024], P(None, 'head'), may hold values from -160 to 160
Outputs:
- readout: bfloat16 [2048, 1024], P(None, 'head')
All inputs are finite; a program needn't handle non-finite values.
Results may differ from a plain program's by a relative error of at most 0.011.
Values may be sent and summed in bfloat16 or wider, within the bound.
No kernel may reach another device: no remote copies, remote signals or barrier semaphores. Data moves between devices by JAX's collectives and lax.ppermute only.
A program may use at most 128 MiB of HBM per device.

v0:
```python
import jax
import jax.numpy as jnp
from jax import lax
from jax.sharding import PartitionSpec as P


def body(patches, w_patch, patch_bias, w_kv, queries):
    embed = jnp.dot(patches, w_patch, preferred_element_type=jnp.float32) + patch_bias
    mean = jnp.mean(embed, axis=-1, keepdims=True)
    var = jnp.mean((embed - mean) * (embed - mean), axis=-1, keepdims=True)
    normed = ((embed - mean) * lax.rsqrt(var + 1e-05)).astype(jnp.bfloat16)
    head_size = queries.shape[1]
    latents = queries.shape[0]
    kv_all = jnp.dot(
        normed, lax.all_gather(w_kv, "head", axis=1, tiled=True), preferred_element_type=jnp.float32
    ).astype(jnp.bfloat16)
    kv = lax.all_to_all(kv_all, "head", split_axis=1, concat_axis=0, tiled=True)
    rows = kv.shape[0]
    block = min(512, rows)
    blocks = kv.reshape(rows // block, block, 2 * head_size)
    scale = float(head_size) ** (-0.5)

    def step(carry, piece):
        run_max, total, accum = carry
        scores = (
            jnp.dot(queries, piece[:, :head_size].T, preferred_element_type=jnp.float32) * scale
        )
        new_max = jnp.maximum(run_max, jnp.max(scores, axis=1))
        factor = jnp.exp(run_max - new_max)
        probs = jnp.exp(scores - new_max[:, None])
        total = total * factor + jnp.sum(probs, axis=1)
        accum = accum * factor[:, None] + jnp.dot(
            probs.astype(jnp.bfloat16), piece[:, head_size:], preferred_element_type=jnp.float32
        )
        return ((new_max, total, accum), None)

    start = (
        jnp.full((latents,), -jnp.inf, jnp.float32),
        jnp.zeros((latents,), jnp.float32),
        jnp.zeros((latents, head_size), jnp.float32),
    )
    (run_max, total, accum), _ = lax.scan(step, start, blocks)
    top = lax.pmax(run_max, "row")
    factor = jnp.exp(run_max - top)
    whole, summed = lax.psum((total * factor, accum * factor[:, None]), "row")
    return (summed / whole[:, None]).astype(jnp.bfloat16)


def solution(mesh):
    placed = (P(("row", "head"), None), P(), P(), P(None, "head"), P(None, "head"))
    return jax.shard_map(
        body, mesh=mesh, in_specs=placed, out_specs=P(None, "head"), check_vma=False
    )
```

profile of v0, /device:TPU:64, one launch (start us, length us, event | category | flops | bytes accessed | tf_op | source)
XLA Modules:
  0.0 447.2 jit_solution(7872800311003511222)
XLA Ops:
  10.2 55.2 %all-gather.2.cloned.1.call-done = bf16[1024,2048]{1,0:T(8,128)(2,1)} async-done(((bf16[1024,128]{1,0:T(8,128)(2,1)}), bf16[1024,2048]{1,0:T(8,128)(2,1)}) %all-gather.2.cloned.1.call-update) | async-done | bytes 4194320 | tf_op jit(solution)/shard_map/all_gather | solution.py:15
  65.4 4.1 fusion.10
  71.1 5.3 %all-to-all-start = ((bf16[384,16,128]{2,0,1:T(8,128)(2,1)}), bf16[384,16,128]{2,0,1:T(8,128)(2,1)}, u32[]{:S(2)}, u32[]{:S(2)}) async-start(bf16[384,16,128]{2,0,1:T(8,128)(2,1)} %bitcast.18), calls=%async_computation | async-start | bytes 3145728 | tf_op jit(solution)/shard_map/all_to_all | solution.py:17
  76.5 36.1 %all-to-all-done = bf16[384,16,128]{2,0,1:T(8,128)(2,1)} async-done(((bf16[384,16,128]{2,0,1:T(8,128)(2,1)}), bf16[384,16,128]{2,0,1:T(8,128)(2,1)}, u32[]{:S(2)}, u32[]{:S(2)}) %all-to-all-start) | async-done | bytes 1572896 | tf_op jit(solution)/shard_map/all_to_all | solution.py:17
  112.5 95.5 %while.15 = (s32[]{:T(128)}, f32[2048]{0:T(1024)S(1)}, f32[2048]{0:T(1024)S(1)}, f32[2048,64]{0,1:T(8,128)S(1)}, bf16[12,512,128]{2,1,0:T(8,128)(2,1)}, /*index=5*/bf16[2048,64]{0,1:T(8,128)(2,1)S(1)}, s32[]{:T(128)}, s32[]{:T(128)}) while((s32[]{:T(128)}, f32[2048]{0:T(1024)S(1)}, f32[2048]{0:T(1024)S(1)}, ...), condition=%wide.region_5.6_spmd.clone, body=%wide.region_2.5_spmd.clone.sunk | while | flops 277227520 | bytes 31326336 | solution.py:42
  113.5 2.6 multiply_reduce_fusion.3
  116.1 3.0 fusion.27
  121.4 2.6 multiply_reduce_fusion.3
  124.0 3.0 fusion.27
  129.4 2.6 multiply_reduce_fusion.3
  132.0 3.0 fusion.27
  137.4 2.6 multiply_reduce_fusion.3
  140.0 3.0 fusion.27
  145.3 2.6 multiply_reduce_fusion.3
  147.9 3.0 fusion.27
  153.3 2.6 multiply_reduce_fusion.3
  155.9 3.0 fusion.27
  161.2 2.6 multiply_reduce_fusion.3
  163.8 3.0 fusion.27
  169.2 2.6 multiply_reduce_fusion.3
  171.8 3.0 fusion.27
  177.1 2.6 multiply_reduce_fusion.3
  179.8 3.0 fusion.27
  185.1 2.6 multiply_reduce_fusion.3
  187.7 3.0 fusion.27
  193.1 2.6 multiply_reduce_fusion.3
  195.7 3.0 fusion.27
  201.0 2.6 multiply_reduce_fusion.3
  203.6 3.0 fusion.27
  208.0 75.6 %pmax.7 = f32[2048]{0:T(1024)S(1)} all-reduce(f32[2048]{0:T(1024)S(1)} %get-tuple-element.40), channel_id=1, replica_groups=mesh['row'=32,'head'=16] {'row'}, use_global_device_ids=true, to_apply=%region_6.7 | all-reduce | flops 2048 | bytes 16384 | tf_op jit(solution)/shard_map/pmax | solution.py:43
  284.6 70.7 %psum.15 = f32[2048]{0:T(1024)S(1)} all-reduce(f32[2048]{0:T(1024)S(1)} %get-tuple-element.77), channel_id=1, replica_groups=mesh['row'=32,'head'=16] {'row'}, use_global_device_ids=true, to_apply=%region_8.9 | all-reduce | flops 2048 | bytes 16384 | tf_op jit(solution)/shard_map/psum | solution.py:45
  355.3 83.3 %all-reduce.2.cloned.1.call-done = f32[2048,64]{0,1:T(8,128)} async-done(((f32[2048,64]{0,1:T(8,128)}), f32[2048,64]{0,1:T(8,128)}) %all-reduce.2.cloned.1.call-update) | async-done | bytes 524304 | tf_op jit(solution)/shard_map/psum | solution.py:45
  (103 shorter events, 35.1 us)
Async XLA Ops:
  6.5 1.4 copy-start
  6.5 58.9 %all-gather.2.cloned.1.call-start = ((), (), s32[]{:S(2)}) async-start(), calls=%async_computation.1 | async-start | bytes 4456448 | tf_op jit(solution)/shard_map/all_gather | solution.py:15
  71.1 41.5 %copy-start.2 = (bf16[2048,64]{0,1:T(8,128)(2,1)S(1)}, bf16[2048,64]{0,1:T(8,128)(2,1)}, u32[]{:S(2)}) copy-start(bf16[2048,64]{0,1:T(8,128)(2,1)} %param.11) | copy-start | bytes 786436
  71.1 41.5 %all-to-all-start = ((bf16[384,16,128]{2,0,1:T(8,128)(2,1)}), bf16[384,16,128]{2,0,1:T(8,128)(2,1)}, u32[]{:S(2)}, u32[]{:S(2)}) async-start(bf16[384,16,128]{2,0,1:T(8,128)(2,1)} %bitcast.18), calls=%async_computation | async-start | bytes 3145728 | tf_op jit(solution)/shard_map/all_to_all | solution.py:17
  76.4 362.2 %all-reduce.2.cloned.1.call-start = ((), (), s32[]{:S(2)}) async-start(), calls=%async_computation.2 | async-start | bytes 1048576 | tf_op jit(solution)/shard_map/psum | solution.py:45
  116.1 3.4 copy-start.1
  124.0 3.4 copy-start.1
  132.0 3.4 copy-start.1
  140.0 3.4 copy-start.1
  147.9 3.4 copy-start.1
  155.9 3.4 copy-start.1
  163.8 3.4 copy-start.1
  171.8 3.4 copy-start.1
  179.8 3.4 copy-start.1
  187.7 3.4 copy-start.1
  195.7 3.4 copy-start.1
  203.6 3.4 copy-start.1
Sparse Core Ops, SparseCore 0:
  9.4 55.9 all-gather.1
  284.7 153.8 all-reduce.1
where the time goes:
time: 448 us; the launch traced here: 447 us
  waiting for transfers between devices  175 us (39%)
  blocking collectives  146 us (33%)
  matrix products  48.6 us (11%)
  other arithmetic  39.7 us (9%)
  local copies, waits for them, and re-layouts  17.9 us (4%)
  between operations  13.5 us (3%)
  starting transfers between devices  5.38 us (1%)
    psum x1, waiting for transfers between devices, body(): whole, summed = lax.psum((total * factor, accum * factor[:, None]), 'row')  83.3 us
    pmax x1, blocking collectives, body(): top = lax.pmax(run_max, 'row')  75.6 us
    psum x1, blocking collectives, body(): whole, summed = lax.psum((total * factor, accum * factor[:, None]), 'row')  70.7 us
    all_gather x1, waiting for transfers between devices, body(): lax.all_gather(w_kv, 'head', axis=1, tiled=True)  55.2 us
    reduce_sum x12, other arithmetic, step(): total = total * factor + jnp.sum(probs, axis=1)  36.6 us
    all_to_all x1, waiting for transfers between devices, body(): kv = lax.all_to_all(kv_all, 'head', split_axis=1, concat_axis=0, tiled=True)  36.1 us
    dot_general x12, matrix products, step(): jnp.dot(queries, piece[:, :head_size].T, preferred_element_type=jnp.float32)  31.3 us
    dot_general x12, matrix products, step(): jnp.dot(probs.astype(jnp.bfloat16), piece[:, head_size:], preferred_eleme...  11.3 us
  transfers between devices with their start and end apart: 3, of which 3 were waited for; matrix products, arithmetic and copies ran while one was open for 1% of the time, Pallas kernels for 0%

commit v1 on v0

--- a/solution.py
+++ b/solution.py
@@ -12,7 +12,11 @@
     head_size = queries.shape[1]
     latents = queries.shape[0]
     kv_all = jnp.dot(
-        normed, lax.all_gather(w_kv, "head", axis=1, tiled=True), preferred_element_type=jnp.float32
+        normed,
+        jnp.concatenate(
+            lax.all_to_all(jnp.stack([w_kv] * lax.axis_size("head")), "head", 0, 0), axis=1
+        ),
+        preferred_element_type=jnp.float32,
     ).astype(jnp.bfloat16)
     kv = lax.all_to_all(kv_all, "head", split_axis=1, concat_axis=0, tiled=True)
     rows = kv.shape[0]

time: 448 us -> 497 us (1.11)
  waiting for transfers between devices: 175 us -> 209 us
  starting transfers between devices: 5.38 us -> 16.9 us
    all_to_all x0 -> x1, waiting for transfers between devices: none -> 90.2 us  [body(): lax.all_to_all(jnp.stack([w_kv] * lax.axis_size('head')), 'head', 0, 0)]
    all_gather x1 -> x0, waiting for transfers between devices: 55.2 us -> none  [body(): lax.all_gather(w_kv, 'head', axis=1, tiled=True)]
    all_to_all x0 -> x1, starting transfers between devices: none -> 10.1 us  [body(): lax.all_to_all(jnp.stack([w_kv] * lax.axis_size('head')), 'head', 0, 0)]
  transfers between devices with their start and end apart: 3 -> 3, of which waited for: 3 -> 3; matrix products, arithmetic and copies ran while one was open for 1% -> 0% of each run, Pallas kernels for 0% -> 0%
where the time goes in v1:
time: 497 us; the launch traced here: 496 us
  waiting for transfers between devices  209 us (42%)
  blocking collectives  147 us (30%)
  matrix products  48.7 us (10%)
  other arithmetic  39.7 us (8%)
  local copies, waits for them, and re-layouts  20.8 us (4%)
  starting transfers between devices  16.9 us (3%)
  between operations  13.5 us (3%)
    all_to_all x1, waiting for transfers between devices, body(): lax.all_to_all(jnp.stack([w_kv] * lax.axis_size('head')), 'head', 0, 0)  90.2 us
    psum x1, waiting for transfers between devices, body(): whole, summed = lax.psum((total * factor, accum * factor[:, None]), 'row')  82.8 us
    pmax x1, blocking collectives, body(): top = lax.pmax(run_max, 'row')  76.3 us
    psum x1, blocking collectives, body(): whole, summed = lax.psum((total * factor, accum * factor[:, None]), 'row')  70.8 us
    reduce_sum x12, other arithmetic, step(): total = total * factor + jnp.sum(probs, axis=1)  36.6 us
    all_to_all x1, waiting for transfers between devices, body(): kv = lax.all_to_all(kv_all, 'head', split_axis=1, concat_axis=0, tiled=True)  36.1 us
    dot_general x12, matrix products, step(): jnp.dot(queries, piece[:, :head_size].T, preferred_element_type=jnp.float32)  31.4 us
    dot_general x12, matrix products, step(): jnp.dot(probs.astype(jnp.bfloat16), piece[:, head_size:], preferred_eleme...  11.3 us
  transfers between devices with their start and end apart: 3, of which 3 were waited for; matrix products, arithmetic and copies ran while one was open for 0% of the time, Pallas kernels for 0%

profile of v1, /device:TPU:64, one launch (start us, length us, event | category | flops | bytes accessed | tf_op | source)
XLA Modules:
  0.0 496.4 jit_solution(1662485368170216970)
XLA Ops:
  10.3 10.1 %all-to-all-start = ((bf16[16,1024,128]{1,2,0:T(8,128)(2,1)}), bf16[16,1024,128]{1,2,0:T(8,128)(2,1)}, u32[]{:S(2)}, u32[]{:S(2)}) async-start(bf16[16,1024,128]{1,2,0:T(8,128)(2,1)} %stack.2), calls=%async_computation | async-start | bytes 8388608 | tf_op jit(solution)/shard_map/all_to_all | solution.py:17
  22.6 90.2 %all-to-all-done = bf16[16,1024,128]{1,2,0:T(8,128)(2,1)} async-done(((bf16[16,1024,128]{1,2,0:T(8,128)(2,1)}), bf16[16,1024,128]{1,2,0:T(8,128)(2,1)}, u32[]{:S(2)}, u32[]{:S(2)}) %all-to-all-start) | async-done | bytes 4194336 | tf_op jit(solution)/shard_map/all_to_all | solution.py:17
  112.8 4.1 fusion.10
  118.5 6.8 %all-to-all-start.1 = ((bf16[384,16,128]{2,0,1:T(8,128)(2,1)}), bf16[384,16,128]{2,0,1:T(8,128)(2,1)}, u32[]{:S(2)}, u32[]{:S(2)}) async-start(bf16[384,16,128]{2,0,1:T(8,128)(2,1)} %bitcast.21), calls=%async_computation.1 | async-start | bytes 3145728 | tf_op jit(solution)/shard_map/all_to_all | solution.py:21
  125.3 36.1 %all-to-all-done.1 = bf16[384,16,128]{2,0,1:T(8,128)(2,1)} async-done(((bf16[384,16,128]{2,0,1:T(8,128)(2,1)}), bf16[384,16,128]{2,0,1:T(8,128)(2,1)}, u32[]{:S(2)}, u32[]{:S(2)}) %all-to-all-start.1) | async-done | bytes 1572896 | tf_op jit(solution)/shard_map/all_to_all | solution.py:21
  161.4 95.5 %while.15 = (s32[]{:T(128)}, f32[2048]{0:T(1024)S(1)}, f32[2048]{0:T(1024)S(1)}, f32[2048,64]{0,1:T(8,128)S(1)}, bf16[12,512,128]{2,1,0:T(8,128)(2,1)}, /*index=5*/bf16[2048,64]{0,1:T(8,128)(2,1)S(1)}, s32[]{:T(128)}, s32[]{:T(128)}) while((s32[]{:T(128)}, f32[2048]{0:T(1024)S(1)}, f32[2048]{0:T(1024)S(1)}, ...), condition=%wide.region_5.6_spmd.clone, body=%wide.region_2.5_spmd.clone.sunk | while | flops 277227520 | bytes 31326344 | solution.py:46
  165.0 3.0 fusion.27
  170.3 2.6 multiply_reduce_fusion.3
  172.9 3.0 fusion.27
  178.2 2.6 multiply_reduce_fusion.3
  180.9 3.0 fusion.27
  186.2 2.6 multiply_reduce_fusion.3
  188.8 3.0 fusion.27
  194.2 2.6 multiply_reduce_fusion.3
  196.8 3.0 fusion.27
  202.1 2.6 multiply_reduce_fusion.3
  204.7 3.0 fusion.27
  210.1 2.6 multiply_reduce_fusion.3
  212.7 3.0 fusion.27
  218.0 2.6 multiply_reduce_fusion.3
  220.7 3.0 fusion.27
  226.0 2.6 multiply_reduce_fusion.3
  228.6 3.0 fusion.27
  233.9 2.6 multiply_reduce_fusion.3
  236.6 3.0 fusion.27
  241.9 2.6 multiply_reduce_fusion.3
  244.5 3.0 fusion.27
  249.9 2.6 multiply_reduce_fusion.3
  252.5 3.0 fusion.27
  256.9 76.3 %pmax.7 = f32[2048]{0:T(1024)S(1)} all-reduce(f32[2048]{0:T(1024)S(1)} %get-tuple-element.40), channel_id=1, replica_groups=mesh['row'=32,'head'=16] {'row'}, use_global_device_ids=true, to_apply=%region_6.7 | all-reduce | flops 2048 | bytes 16384 | tf_op jit(solution)/shard_map/pmax | solution.py:47
  334.1 70.8 %psum.15 = f32[2048]{0:T(1024)S(1)} all-reduce(f32[2048]{0:T(1024)S(1)} %get-tuple-element.77), channel_id=1, replica_groups=mesh['row'=32,'head'=16] {'row'}, use_global_device_ids=true, to_apply=%region_8.9 | all-reduce | flops 2048 | bytes 16384 | tf_op jit(solution)/shard_map/psum | solution.py:49
  404.9 82.8 %all-reduce.2.cloned.1.call-done = f32[2048,64]{0,1:T(8,128)} async-done(((f32[2048,64]{0,1:T(8,128)}), f32[2048,64]{0,1:T(8,128)}) %all-reduce.2.cloned.1.call-update) | async-done | bytes 524304 | tf_op jit(solution)/shard_map/psum | solution.py:49
  (106 shorter events, 39.9 us)
Async XLA Ops:
  6.5 13.8 %copy-start = (bf16[768,1024]{1,0:T(8,128)(2,1)S(1)}, bf16[768,1024]{1,0:T(8,128)(2,1)}, u32[]{:S(2)}) copy-start(bf16[768,1024]{1,0:T(8,128)(2,1)} %param.8) | copy-start | bytes 4718596
  10.3 10.1 %copy-start.3 = (f32[1024]{0:T(1024)S(1)}, f32[1024]{0:T(1024)}, u32[]{:S(2)}) copy-start(f32[1024]{0:T(1024)} %param.9) | copy-start | bytes 12292
  10.3 102.6 %all-to-all-start = ((bf16[16,1024,128]{1,2,0:T(8,128)(2,1)}), bf16[16,1024,128]{1,2,0:T(8,128)(2,1)}, u32[]{:S(2)}, u32[]{:S(2)}) async-start(bf16[16,1024,128]{1,2,0:T(8,128)(2,1)} %stack.2), calls=%async_computation | async-start | bytes 8388608 | tf_op jit(solution)/shard_map/all_to_all | solution.py:17
  118.5 42.9 %copy-start.2 = (bf16[2048,64]{0,1:T(8,128)(2,1)S(1)}, bf16[2048,64]{0,1:T(8,128)(2,1)}, u32[]{:S(2)}) copy-start(bf16[2048,64]{0,1:T(8,128)(2,1)} %param.11) | copy-start | bytes 786436
  118.5 42.9 %all-to-all-start.1 = ((bf16[384,16,128]{2,0,1:T(8,128)(2,1)}), bf16[384,16,128]{2,0,1:T(8,128)(2,1)}, u32[]{:S(2)}, u32[]{:S(2)}) async-start(bf16[384,16,128]{2,0,1:T(8,128)(2,1)} %bitcast.21), calls=%async_computation.1 | async-start | bytes 3145728 | tf_op jit(solution)/shard_map/all_to_all | solution.py:21
  125.3 362.5 %all-reduce.2.cloned.1.call-start = ((), (), s32[]{:S(2)}) async-start(), calls=%async_computation.2 | async-start | bytes 1048576 | tf_op jit(solution)/shard_map/psum | solution.py:49
  165.0 3.4 copy-start.1
  172.9 3.4 copy-start.1
  180.9 3.4 copy-start.1
  188.8 3.4 copy-start.1
  196.8 3.4 copy-start.1
  204.7 3.4 copy-start.1
  212.7 3.4 copy-start.1
  220.7 3.4 copy-start.1
  228.6 3.4 copy-start.1
  236.6 3.4 copy-start.1
  244.5 3.4 copy-start.1
  252.5 3.4 copy-start.1
Sparse Core Ops, SparseCore 0:
  334.3 153.4 all-reduce.1
